TPU v7x, 32 devices: a whole 2x2x4 slice. The times are simulated.
32 devices in a mesh: dp: 16 (over z, x, core), mp: 2 (over y).
Axes of the slice: x: 2, y: 2, z: 4, core: 2. Of those that a mesh axis runs over, the one named last changes fastest.
Arguments:
- tokens: bfloat16 [12544, 768], P(('dp', 'mp')), may hold values from -6 to 6
- tissue: int32 [16, 784], P('dp'), may hold values from 0 to 1, as said below
- first_gain: float32 [768], replicated, may hold values from 0.5 to 1.5
- first_shift: float32 [768], replicated, may hold values from -3 to 3
- w_query: bfloat16 [768, 768], P(None, 'mp'), may hold values from -0.21875 to 0.21875
- b_query: float32 [768], P('mp'), may hold values from -3 to 3
- w_key: bfloat16 [768, 768], P(None, 'mp'), may hold values from -0.21875 to 0.21875
- w_value: bfloat16 [768, 768], P(None, 'mp'), may hold values from -0.21875 to 0.21875
- b_value: float32 [768], P('mp'), may hold values from -3 to 3
- w_output: bfloat16 [768, 768], P('mp'), may hold values from -1.75 to 1.75
- b_output: float32 [768], replicated, may hold values from -3 to 3
- second_gain: float32 [768], replicated, may hold values from 0.5 to 1.5
- second_shift: float32 [768], replicated, may hold values from -3 to 3
- w_upward: bfloat16 [768, 3072], P(None, 'mp'), may hold values from -0.21875 to 0.21875
- b_upward: float32 [3072], P('mp'), may hold values from -3 to 3
- w_down: bfloat16 [3072, 768], P('mp'), may hold values from -0.109375 to 0.109375
- b_down: float32 [768], replicated, may hold values from -3 to 3
- cotangent: bfloat16 [12544, 768], P(('dp', 'mp')), may hold values from -6 to 6
Outputs:
- output: bfloat16 [12544, 768], P(('dp', 'mp'))
- grad_tokens: float32 [12544, 768], P(('dp', 'mp'))
- grad_first_gain: float32 [768], replicated
- grad_first_shift: float32 [768], replicated
- grad_w_query: float32 [768, 768], P(None, 'mp')
- grad_b_query: float32 [768], P('mp')
- grad_w_key: float32 [768, 768], P(None, 'mp')
- grad_w_value: float32 [768, 768], P(None, 'mp')
- grad_b_value: float32 [768], P('mp')
- grad_w_output: float32 [768, 768], P('mp')
- grad_b_output: float32 [768], replicated
- grad_second_gain: float32 [768], replicated
- grad_second_shift: float32 [768], replicated
- grad_w_upward: float32 [768, 3072], P(None, 'mp')
- grad_b_upward: float32 [3072], P('mp')
- grad_w_down: float32 [3072, 768], P('mp')
- grad_b_down: float32 [768], replicated
Inputs may be any that keep to these rules, and one draw needn't show every extreme that they name: `tissue`: every image has from 196 to 784 patches marked 1, in no particular places.
All inputs are finite; a program needn't handle non-finite values.
Results may differ from a plain program's by a relative error of at most 0.015.
Values may be sent and summed in bfloat16 or wider, within the bound.
No kernel may reach another device: no remote copies, remote signals or barrier semaphores. Data moves between devices by JAX's collectives and lax.ppermute only.
A program may use at most 128 MiB of HBM per device.

v0:
```python
import jax
import jax.numpy as jnp
from jax import lax
from jax.sharding import PartitionSpec as P

HEAD = 64
epsilon = 1e-06
masked_score = -1e30


def normalize(values, gain, shift):
    average = jnp.mean(values, axis=-1, keepdims=True)
    centred = values - average
    spread = jnp.mean(centred * centred, axis=-1, keepdims=True)
    return centred * lax.rsqrt(spread + epsilon) * gain + shift


def exact_gelu(values):
    return jax.nn.gelu(values, approximate=False)


def head_layer(
    tokens,
    tissue,
    first_gain,
    first_shift,
    w_query,
    b_query,
    w_key,
    w_value,
    b_value,
    w_output,
    b_output,
    second_gain,
    second_shift,
    w_upward,
    b_upward,
    w_down,
    b_down,
    cotangent,
):
    images = tissue.shape[0]
    patches = tissue.shape[1]
    width_local = w_query.shape[1]
    heads_local = width_local // HEAD
    head_shape = (images, patches, heads_local, HEAD)
    group_rows = images * patches
    scale = HEAD ** (-0.5)
    inputs = tokens.astype(jnp.float32)
    normed1 = normalize(inputs, first_gain, first_shift).astype(jnp.bfloat16)
    gathered1 = lax.all_gather(normed1, "mp", axis=0, tiled=True)
    w_stack = jnp.concatenate([w_query, w_key, w_value], axis=1)
    b_stack = jnp.concatenate([b_query, jnp.zeros_like(b_query), b_value])
    stacked = (jnp.dot(gathered1, w_stack, preferred_element_type=jnp.float32) + b_stack).astype(
        jnp.bfloat16
    )
    queries = stacked[:, :width_local].reshape(head_shape)
    key_rows = stacked[:, width_local : 2 * width_local].reshape(head_shape)
    value_rows = stacked[:, 2 * width_local :].reshape(head_shape)
    valid_keys = (tissue > 0)[:, None, None, :]

    def masked_scores():
        raw_scores = (
            jnp.einsum("ipha,iqha->ihpq", queries, key_rows, preferred_element_type=jnp.float32)
            * scale
        )
        return jnp.where(valid_keys, raw_scores, masked_score)

    scores = masked_scores()
    highest = jnp.max(scores, axis=-1, keepdims=True)
    log_total = highest + jnp.log(jnp.sum(jnp.exp(scores - highest), axis=-1, keepdims=True))
    chance_low = jnp.exp(scores - log_total).astype(jnp.bfloat16)
    context = jnp.einsum(
        "ihpq,iqha->ipha", chance_low, value_rows, preferred_element_type=jnp.float32
    )
    context = context.reshape(group_rows, width_local).astype(jnp.bfloat16)
    part_rows = context
    attention = (
        lax.psum_scatter(
            jnp.dot(part_rows, w_output, preferred_element_type=jnp.float32).astype(jnp.bfloat16),
            "mp",
            scatter_dimension=0,
            tiled=True,
        ).astype(jnp.float32)
        + b_output
    )
    hidden1 = inputs + attention
    normed2 = normalize(hidden1, second_gain, second_shift).astype(jnp.bfloat16)
    gathered2 = lax.all_gather(normed2, "mp", axis=0, tiled=True)
    pre_gelu = jnp.dot(gathered2, w_upward, preferred_element_type=jnp.float32) + b_upward
    activated = exact_gelu(pre_gelu).astype(jnp.bfloat16)
    part_rows = activated
    branch_mlp = (
        lax.psum_scatter(
            jnp.dot(part_rows, w_down, preferred_element_type=jnp.float32).astype(jnp.bfloat16),
            "mp",
            scatter_dimension=0,
            tiled=True,
        ).astype(jnp.float32)
        + b_down
    )
    output = (hidden1 + branch_mlp).astype(jnp.bfloat16)
    grad_rows = lax.all_gather(cotangent, "mp", axis=0, tiled=True)
    grad_down = jnp.einsum("gf,gd->fd", activated, grad_rows, preferred_element_type=jnp.float32)
    grad_active = jnp.einsum("gd,fd->gf", grad_rows, w_down, preferred_element_type=jnp.float32)
    gelu_back = jax.vjp(exact_gelu, pre_gelu)[1]
    grad_pre = gelu_back(grad_active)[0].astype(jnp.bfloat16)
    grad_upward = jnp.einsum("gd,gf->df", gathered2, grad_pre, preferred_element_type=jnp.float32)
    grad_bupward = jnp.sum(grad_pre.astype(jnp.float32), axis=0)
    part_rows = grad_pre
    grad_normed2 = lax.psum_scatter(
        jnp.einsum("gf,df->gd", part_rows, w_upward, preferred_element_type=jnp.float32).astype(
            jnp.bfloat16
        ),
        "mp",
        scatter_dimension=0,
        tiled=True,
    ).astype(jnp.float32)
    norm2_back = jax.vjp(normalize, hidden1, second_gain, second_shift)[1]
    grad_hidden, grad_gain2, grad_shift2 = norm2_back(grad_normed2)
    cotangent_f = cotangent.astype(jnp.float32)
    grad_hidden = grad_hidden + cotangent_f
    grad_bdown = jnp.sum(cotangent_f, axis=0)
    grad_branch = grad_hidden.astype(jnp.bfloat16)
    grad_boutput = jnp.sum(grad_branch.astype(jnp.float32), axis=0)
    grad_columns = lax.all_gather(grad_branch, "mp", axis=0, tiled=True)
    grad_woutput = jnp.einsum(
        "gc,gd->cd", context, grad_columns, preferred_element_type=jnp.float32
    )
    grad_context = jnp.einsum(
        "gd,cd->gc", grad_columns, w_output, preferred_element_type=jnp.float32
    )
    grad_context = grad_context.astype(jnp.bfloat16).reshape(head_shape)
    chances = jnp.exp(masked_scores() - log_total)
    grad_chances = jnp.einsum(
        "ipha,iqha->ihpq", grad_context, value_rows, preferred_element_type=jnp.float32
    )
    grad_value = jnp.einsum(
        "ihpq,ipha->iqha",
        chances.astype(jnp.bfloat16),
        grad_context,
        preferred_element_type=jnp.float32,
    ).astype(jnp.bfloat16)
    grad_scores = chances * (grad_chances - jnp.sum(chances * grad_chances, axis=-1, keepdims=True))
    grad_scores = grad_scores.astype(jnp.bfloat16)
    grad_query = (
        jnp.einsum("ihpq,iqha->ipha", grad_scores, key_rows, preferred_element_type=jnp.float32)
        * scale
    ).astype(jnp.bfloat16)
    grad_key = (
        jnp.einsum("ihpq,ipha->iqha", grad_scores, queries, preferred_element_type=jnp.float32)
        * scale
    ).astype(jnp.bfloat16)
    grad_stack = jnp.concatenate(
        [
            grad_query.reshape(group_rows, width_local),
            grad_key.reshape(group_rows, width_local),
            grad_value.reshape(group_rows, width_local),
        ],
        axis=1,
    )
    grad_wstack = jnp.einsum("gd,gc->dc", gathered1, grad_stack, preferred_element_type=jnp.float32)
    stack_sums = jnp.sum(grad_stack.astype(jnp.float32), axis=0)
    part_rows = grad_stack
    grad_normed1 = lax.psum_scatter(
        jnp.einsum("gc,dc->gd", part_rows, w_stack, preferred_element_type=jnp.float32).astype(
            jnp.bfloat16
        ),
        "mp",
        scatter_dimension=0,
        tiled=True,
    ).astype(jnp.float32)
    norm1_back = jax.vjp(normalize, inputs, first_gain, first_shift)[1]
    grad_inputs, grad_gain1, grad_shift1 = norm1_back(grad_normed1)
    grad_tokens = grad_hidden + grad_inputs
    weight_grads = (
        grad_wstack[:, :width_local],
        stack_sums[:width_local],
        grad_wstack[:, width_local : 2 * width_local],
        grad_wstack[:, 2 * width_local :],
        stack_sums[2 * width_local :],
        grad_woutput,
        grad_upward,
        grad_bupward,
        grad_down,
    )
    small_grads = (grad_gain1, grad_shift1, grad_boutput, grad_gain2, grad_shift2, grad_bdown)
    return (output, grad_tokens, small_grads, weight_grads)


def local(
    tokens,
    tissue,
    first_gain,
    first_shift,
    w_query,
    b_query,
    w_key,
    w_value,
    b_value,
    w_output,
    b_output,
    second_gain,
    second_shift,
    w_upward,
    b_upward,
    w_down,
    b_down,
    cotangent,
):
    arguments = (
        tokens,
        tissue,
        first_gain,
        first_shift,
        w_query,
        b_query,
        w_key,
        w_value,
        b_value,
        w_output,
        b_output,
        second_gain,
        second_shift,
        w_upward,
        b_upward,
        w_down,
        b_down,
        cotangent,
    )
    output, grad_tokens, small_grads, weight_grads = head_layer(*arguments)
    (
        grad_wquery,
        grad_bquery,
        grad_wkey,
        grad_wvalue,
        grad_bvalue,
        grad_woutput,
        grad_upward,
        grad_bupward,
        grad_down,
    ) = weight_grads
    (
        grad_wquery,
        grad_bquery,
        grad_wkey,
        grad_wvalue,
        grad_bvalue,
        grad_woutput,
        grad_upward,
        grad_bupward,
        grad_down,
    ) = lax.psum(
        (
            grad_wquery,
            grad_bquery,
            grad_wkey,
            grad_wvalue,
            grad_bvalue,
            grad_woutput,
            grad_upward,
            grad_bupward,
            grad_down,
        ),
        "dp",
    )
    grad_gain1, grad_shift1, grad_boutput, grad_gain2, grad_shift2, grad_bdown = small_grads
    grad_gain1, grad_shift1, grad_boutput, grad_gain2, grad_shift2, grad_bdown = lax.psum(
        (grad_gain1, grad_shift1, grad_boutput, grad_gain2, grad_shift2, grad_bdown), ("dp", "mp")
    )
    return (
        output,
        grad_tokens,
        grad_gain1,
        grad_shift1,
        grad_wquery,
        grad_bquery,
        grad_wkey,
        grad_wvalue,
        grad_bvalue,
        grad_woutput,
        grad_boutput,
        grad_gain2,
        grad_shift2,
        grad_upward,
        grad_bupward,
        grad_down,
        grad_bdown,
    )


def solution(mesh):
    in_specs = (
        P(("dp", "mp"), None),
        P("dp", None),
        P(),
        P(),
        P(None, "mp"),
        P("mp"),
        P(None, "mp"),
        P(None, "mp"),
        P("mp"),
        P("mp", None),
        P(),
        P(),
        P(),
        P(None, "mp"),
        P("mp"),
        P("mp", None),
        P(),
        P(("dp", "mp"), None),
    )
    out_specs = (
        P(("dp", "mp"), None),
        P(("dp", "mp"), None),
        P(),
        P(),
        P(None, "mp"),
        P("mp"),
        P(None, "mp"),
        P(None, "mp"),
        P("mp"),
        P("mp", None),
        P(),
        P(),
        P(),
        P(None, "mp"),
        P("mp"),
        P("mp", None),
        P(),
    )
    return jax.shard_map(local, mesh=mesh, in_specs=in_specs, out_specs=out_specs, check_vma=False)
```

profile of v0, /device:TPU:0, one launch (start us, length us, event | category | flops | bytes accessed | tf_op | source)
XLA Modules:
  0.0 604.4 jit_solution(9951858389328352436)
XLA Ops:
  7.3 1.4 convert_reduce_fusion.4
  8.7 1.4 fusion.22
  10.1 2.2 fusion.20
  12.4 1.3 pad_maximum_fusion.1
  14.5 0.9 constant_dynamic-update-slice_fusion.2
  16.2 0.9 constant_dynamic-update-slice_fusion
  17.1 21.1 %all-gather.5.cloned.1.call-done = bf16[784,768]{1,0:T(8,128)(2,1)} async-done(((bf16[392,768]{1,0:T(8,128)(2,1)}), bf16[784,768]{1,0:T(8,128)(2,1)}) %all-gather.5.cloned.1.call-update) | async-done | bytes 1204240 | tf_op jit(solution)/shard_map/all_gather | solution.py:51
  38.2 3.5 fusion.8
  41.8 1.2 fusion.37
  43.0 2.2 copy.47
  45.2 2.2 copy.48
  47.4 1.1 copy.49
  48.5 10.4 %fusion = (f32[6,784]{1,0:T(8,128)S(1)}, f32[6,784,784]{1,2,0:T(8,128)}) fusion(pred[784]{0:T(1024)(128)(4,1)S(1)} %compare_reduce_fusion, bf16[784,6,64]{0,2,1:T(8,128)(2,1)} %bitcast.58, bf16[784,6,64]{0,2,1:T(8,128)(2,1)} %bitcast.60), kind=kOutput, calls=%fused_computation.5 | convolution fusion | flops 483114912 | bytes 15975568 | tf_op jit(solution)/shard_map/ipha,iqha->ihpq/dot_general | solution.py:64
  58.9 9.3 %exponential_reduce_fusion = f32[6,784]{1,0:T(8,128)S(1)} fusion(f32[6,784,784]{1,2,0:T(8,128)} %get-tuple-element.58, f32[6,784]{1,0:T(8,128)S(1)} %get-tuple-element.57, pred[784]{0:T(1024)(128)(4,1)S(1)} %compare_reduce_fusion), kind=kLoop, calls=%fused_computation.3 | loop fusion | flops 14747040 | bytes 14790160 | tf_op jit(solution)/shard_map/reduce_sum | solution.py:71
  68.2 8.2 %fusion.1 = bf16[6,784,784]{1,2,0:T(8,128)(2,1)S(1)} fusion(f32[6,784,784]{1,2,0:T(8,128)} %get-tuple-element.58, f32[6,784]{1,0:T(8,128)S(1)} %log_add_fusion, pred[784]{0:T(1024)(128)(4,1)S(1)} %compare_reduce_fusion), kind=kLoop, calls=%fused_computation.6 | loop fusion | flops 14751744 | bytes 22147216 | tf_op jit(solution)/shard_map/convert_element_type | solution.py:72
  76.5 1.7 convolution_convert_fusion.5
  78.2 1.5 copy-done.2
  80.6 1.8 convolution_convert_fusion.1
  82.5 22.1 %reduce-scatter.5.cloned.1.call-done = bf16[392,768]{1,0:T(8,128)(2,1)} async-done(((bf16[784,768]{1,0:T(8,128)(2,1)}), bf16[392,768]{1,0:T(8,128)(2,1)}) %reduce-scatter.5.cloned.1.call-update) | async-done | bytes 602128 | tf_op jit(solution)/shard_map/reduce_scatter | solution.py:79
  104.7 1.4 fusion.27
  106.1 1.4 multiply_reduce_fusion.1
  107.5 1.2 add_convert_fusion.2
  109.4 22.6 %all-gather.7.cloned.1.call-done = bf16[784,768]{1,0:T(8,128)(2,1)} async-done(((bf16[392,768]{1,0:T(8,128)(2,1)}), bf16[784,768]{1,0:T(8,128)(2,1)}) %all-gather.7.cloned.1.call-update) | async-done | bytes 1204240 | tf_op jit(solution)/shard_map/all_gather | solution.py:89
  132.0 6.3 %fusion.39 = f32[784,1536]{1,0:T(8,128)} fusion(bf16[784,768]{1,0:T(8,128)(2,1)} %all-gather.7.cloned.1.call-done, bf16[768,1536]{1,0:T(8,128)(2,1)} %param.31), kind=kOutput, calls=%fused_computation.98 | convolution fusion | flops 1849688064 | bytes 8380416 | tf_op jit(solution)/shard_map/dot_general | solution.py:90
  138.3 18.2 %all-gather.9.cloned.1.call-done = bf16[784,768]{1,0:T(8,128)(2,1)} async-done(((bf16[392,768]{1,0:T(8,128)(2,1)}), bf16[784,768]{1,0:T(8,128)(2,1)}) %all-gather.9.cloned.1.call-update) | async-done | bytes 1204240 | tf_op jit(solution)/shard_map/all_gather | solution.py:103
  156.5 15.6 %convert_reduce_fusion = (f32[1536]{0:T(1024)S(1)}, bf16[784,1536]{1,0:T(8,128)(2,1)S(1)}, f32[784,1536]{1,0:T(8,128)}) fusion(f32[784,1536]{1,0:T(8,128)} %fusion.39, f32[1536]{0:T(1024)S(1)} %copy-done.39, bf16[784,768]{1,0:T(8,128)(2,1)} %all-gather.9.cloned.1.call-done, bf16[1536,768]{1,0:T(8,128)(2,1)S(1)} %copy-done), kind=kOutput, calls=%fused_computation.9 | convolution fusion | flops 1940003328 | bytes 15618048 | tf_op jit(solution)/shard_map/gd,fd->gf/dot_general | solution.py:105
  172.0 1.4 copy-done.21
  173.5 3.1 convolution_convert_fusion.2
  176.6 5.0 multiply_convert_fusion.1
  181.7 1.4 copy-done.19
  183.1 3.1 convolution_convert_fusion.3
  186.3 12.5 %reduce-scatter.9.cloned.1.call-done = bf16[392,768]{1,0:T(8,128)(2,1)} async-done(((bf16[784,768]{1,0:T(8,128)(2,1)}), bf16[392,768]{1,0:T(8,128)(2,1)}) %reduce-scatter.9.cloned.1.call-update) | async-done | bytes 602128 | tf_op jit(solution)/shard_map/reduce_scatter | solution.py:111
  198.7 1.9 fusion.24
  200.6 22.3 %reduce-scatter.7.cloned.1.call-done = bf16[392,768]{1,0:T(8,128)(2,1)} async-done(((bf16[784,768]{1,0:T(8,128)(2,1)}), bf16[392,768]{1,0:T(8,128)(2,1)}) %reduce-scatter.7.cloned.1.call-update) | async-done | bytes 602128 | tf_op jit(solution)/shard_map/reduce_scatter | solution.py:94
  222.9 2.7 fusion.35
  225.7 2.1 convert_reduce_fusion.6
  228.1 23.0 %all-gather.11.cloned.1.call-done = bf16[784,768]{1,0:T(8,128)(2,1)} async-done(((bf16[392,768]{1,0:T(8,128)(2,1)}), bf16[784,768]{1,0:T(8,128)(2,1)}) %all-gather.11.cloned.1.call-update) | async-done | bytes 1204240 | tf_op jit(solution)/shard_map/all_gather | solution.py:126
  251.1 2.2 convolution_convert_fusion.6
  253.3 1.1 copy.51
  254.4 6.4 %convolution_convert_fusion.4 = bf16[6,64,784]{2,1,0:T(8,128)(2,1)S(1)} fusion(bf16[784,6,64]{0,2,1:T(8,128)(2,1)} %bitcast.64, bf16[6,784,784]{1,2,0:T(8,128)(2,1)} %copy-done.2), kind=kOutput, calls=%fused_computation.57 | convolution fusion | flops 472356864 | bytes 8580096 | tf_op jit(solution)/shard_map/ihpq,ipha->iqha/dot_general | solution.py:138
  260.9 12.1 %multiply_reduce_fusion = (f32[6,784]{1,0:T(8,128)S(1)}, f32[6,784,784]{1,2,0:T(8,128)}) fusion(f32[6,784,784]{1,2,0:T(8,128)} %get-tuple-element.58, f32[6,784]{1,0:T(8,128)S(1)} %log_add_fusion, pred[784]{0:T(1024)(128)(4,1)S(1)} %compare_reduce_fusion, bf16[784,6,64]{0,2,1:T(8,128)(2,1)S(1)} %bitcast.65, bf16[784,6,64]{0,2,1:T(8,128)(2,1)S(1)} %bitcast.63), kind=kOutput, calls=%fused_computation.1 | convolution fusion | flops 490490784 | bytes 30746128 | tf_op jit(solution)/shard_map/ipha,iqha->ihpq/dot_general | solution.py:135
  273.0 12.3 %multiply_convert_fusion = bf16[6,784,784]{1,2,0:T(8,128)(2,1)S(1)} fusion(f32[6,784,784]{1,2,0:T(8,128)} %get-tuple-element.60, f32[6,784,784]{1,2,0:T(8,128)} %get-tuple-element.58, f32[6,784]{1,0:T(8,128)S(1)} %get-tuple-element.59, f32[6,784]{1,0:T(8,128)S(1)} %log_add_fusion, pred[784]{0:T(1024)(128)(4,1)S(1)} %compare_reduce_fusion), kind=kLoop, calls=%fused_computation | loop fusion | flops 22127616 | bytes 36917776 | tf_op jit(solution)/shard_map/convert_element_type | solution.py:145
  285.3 2.8 fusion.17
  288.1 1.7 fusion.16
  290.6 4.5 convolution_convert_fusion
  295.5 7.0 %fusion.41 = f32[768,1536]{1,0:T(8,128)} fusion(bf16[784,768]{1,0:T(8,128)(2,1)} %all-gather.7.cloned.1.call-done, bf16[784,1536]{1,0:T(8,128)(2,1)} %copy-done.21), kind=kOutput, calls=%fused_computation.100 | convolution fusion | flops 1849688064 | bytes 8331264 | tf_op jit(solution)/shard_map/gd,gf->df/dot_general | solution.py:108
  302.5 4.3 fusion.42
  306.9 1.8 fusion.40
  309.2 2.2 fusion.32
  311.5 1.9 fusion.36
  313.4 2.0 convert_reduce_fusion.1
  315.3 64.0 %all-reduce.1 = (f32[384]{0:T(512)}, f32[384]{0:T(512)}, f32[1536]{0:T(1024)}) all-reduce(f32[384]{0:T(512)S(1)} %get-tuple-element.56, f32[384]{0:T(512)S(1)} %get-tuple-element.55, f32[1536]{0:T(1024)S(1)} %get-tuple-element.39), channel_id=1, replica_groups=mesh['dp'=16,'mp'=2] {'dp'}, use_global_device_ids=true, to_apply=%region_21.22 | all-reduce | flops 2304 | bytes 18432 | tf_op jit(solution)/shard_map/psum | solution.py:253
  379.4 1.6 convert_reduce_fusion.2
  381.0 1.9 fusion.25
  382.9 2.7 convert_reduce_fusion.5
  385.6 39.1 %all-reduce = (f32[768]{0:T(1024)}, f32[768]{0:T(1024)}, f32[768]{0:T(1024)}, f32[768]{0:T(1024)}, f32[768]{0:T(1024)}, /*index=5*/f32[768]{0:T(1024)}) all-reduce(f32[768]{0:T(1024)S(1)} %get-tuple-element.19, f32[768]{0:T(1024)S(1)} %get-tuple-element.22, ...), channel_id=1, replica_groups=mesh['dp'=16,'mp'=2] {'dp','mp'}, use_global_device_ids=true, to_apply=%region_16.17 | all-reduce | flops 4608 | bytes 36864 | tf_op jit(solution)/shard_map/psum | solution.py:268
  424.7 160.7 %all-reduce.5.cloned.1.call-done = (f32[768,384]{1,0:T(8,128)}, f32[768,384]{1,0:T(8,128)}, f32[768,384]{1,0:T(8,128)}, f32[384,768]{1,0:T(8,128)}, f32[768,1536]{1,0:T(8,128)}, /*index=5*/f32[1536,768]{1,0:T(8,128)}) async-done(((f32[768,384]{1,0:T(8,128)}, f32[768,384]{1,0:T(8,128)}, f32[768,384]{1,0:T(8,128)}, f32[384,768]{1,0:T(8,128)}, f32[768,1536]{1,0:T(8,128)}, /*index=5*/f32[1536,768]{1,0:T(8,128)}), ...) | async-done | bytes 14155792 | tf_op jit(solution)/shard_map/psum | solution.py:253
  585.4 2.5 copy.67
  587.9 1.0 copy.68
  588.9 1.0 copy.69
  590.0 1.0 copy.70
  591.5 2.2 copy.71
  594.0 2.4 copy.72
  596.4 1.0 copy-done.1
  (129 shorter events, 6.5 us)
Async XLA Ops:
  7.2 149.3 %copy-start = (bf16[1536,768]{1,0:T(8,128)(2,1)S(1)}, bf16[1536,768]{1,0:T(8,128)(2,1)}, u32[]{:S(2)}) copy-start(bf16[1536,768]{1,0:T(8,128)(2,1)} %param.33) | copy-start | bytes 7077892
  7.2 5.2 copy-start.42
  7.2 7.2 %copy-start.27 = (bf16[768,384]{1,0:T(8,128)(2,1)S(1)}, bf16[768,384]{1,0:T(8,128)(2,1)}, u32[]{:S(2)}) copy-start(bf16[768,384]{1,0:T(8,128)(2,1)} %param.22) | copy-start | bytes 1769476
  7.2 8.1 %copy-start.28 = (bf16[768,384]{1,0:T(8,128)(2,1)S(1)}, bf16[768,384]{1,0:T(8,128)(2,1)}, u32[]{:S(2)}) copy-start(bf16[768,384]{1,0:T(8,128)(2,1)} %param.24) | copy-start | bytes 1769476
  7.2 31.0 %all-gather.5.cloned.1.call-start = ((), (), s32[]{:S(2)}) async-start(), calls=%async_computation.4 | async-start | bytes 1806336 | tf_op jit(solution)/shard_map/all_gather | solution.py:51
  8.7 7.5 %copy-start.31 = (f32[392]{0:T(512)}, f32[392]{0:T(512)S(1)}, u32[]{:S(2)}) copy-start(f32[392]{0:T(512)S(1)} %broadcast_multiply_fusion.1) | copy-start | bytes 4708
  10.1 7.0 %copy-start.37 = (f32[392]{0:T(512)}, f32[392]{0:T(512)S(1)}, u32[]{:S(2)}) copy-start(f32[392]{0:T(512)S(1)} %fusion.22) | copy-start | bytes 4708
  10.1 7.0 %copy-start.35 = (f32[392]{0:T(512)}, f32[392]{0:T(512)S(1)}, u32[]{:S(2)}) copy-start(f32[392]{0:T(512)S(1)} %fusion.30) | copy-start | bytes 4708
  12.3 92.3 %reduce-scatter.5.cloned.1.call-start = ((), (), s32[]{:S(2)}) async-start(), calls=%async_computation.5 | async-start | bytes 1806336 | tf_op jit(solution)/shard_map/reduce_scatter | solution.py:79
  12.4 3.9 copy-start.29
  68.2 8.3 %copy-start.8 = (bf16[784,384]{0,1:T(8,128)(2,1)S(1)}, bf16[784,384]{0,1:T(8,128)(2,1)}, u32[]{:S(2)}) copy-start(bf16[784,384]{0,1:T(8,128)(2,1)} %copy.47) | copy-start | bytes 1806340
  76.5 3.3 copy-start.2
  76.5 4.1 copy-start.47
  79.7 0.9 copy-start.25
  79.7 24.9 %copy-start.3 = (bf16[392,768]{1,0:T(8,128)(2,1)S(1)}, bf16[392,768]{1,0:T(8,128)(2,1)}, u32[]{:S(2)}) copy-start(bf16[392,768]{1,0:T(8,128)(2,1)} %param.18) | copy-start | bytes 1806340
  79.7 24.9 %copy-start.30 = (f32[768]{0:T(1024)S(1)}, f32[768]{0:T(1024)}, u32[]{:S(2)}) copy-start(f32[768]{0:T(1024)} %param.28) | copy-start | bytes 9220
  82.4 25.1 %copy-start.34 = (f32[768]{0:T(1024)S(1)}, f32[768]{0:T(1024)}, u32[]{:S(2)}) copy-start(f32[768]{0:T(1024)} %param.29) | copy-start | bytes 9220
  82.4 25.1 %copy-start.40 = (f32[768]{0:T(1024)S(1)}, f32[768]{0:T(1024)}, u32[]{:S(2)}) copy-start(f32[768]{0:T(1024)} %param.30) | copy-start | bytes 9220
  82.5 49.5 %all-gather.7.cloned.1.call-start = ((), (), s32[]{:S(2)}) async-start(), calls=%async_computation.6 | async-start | bytes 1806336 | tf_op jit(solution)/shard_map/all_gather | solution.py:89
  104.7 2.9 copy-start.4
  108.7 47.7 %all-gather.9.cloned.1.call-start = ((), (), s32[]{:S(2)}) async-start(), calls=%async_computation.8 | async-start | bytes 1806336 | tf_op jit(solution)/shard_map/all_gather | solution.py:103
  109.3 47.1 %copy-start.39 = (f32[1536]{0:T(1024)S(1)}, f32[1536]{0:T(1024)}, u32[]{:S(2)}) copy-start(f32[1536]{0:T(1024)} %param.32) | copy-start | bytes 18436
  109.3 89.4 %reduce-scatter.9.cloned.1.call-start = ((), (), s32[]{:S(2)}) async-start(), calls=%async_computation.9 | async-start | bytes 1806336 | tf_op jit(solution)/shard_map/reduce_scatter | solution.py:111
  156.5 17.0 %copy-start.43 = (bf16[768,1536]{1,0:T(8,128)(2,1)S(1)}, bf16[768,1536]{1,0:T(8,128)(2,1)}, u32[]{:S(2)}) copy-start(bf16[768,1536]{1,0:T(8,128)(2,1)} %param.31) | copy-start | bytes 7077892
  172.0 1.4 copy-start.21
  176.6 46.3 %reduce-scatter.7.cloned.1.call-start = ((), (), s32[]{:S(2)}) async-start(), calls=%async_computation.7 | async-start | bytes 1806336 | tf_op jit(solution)/shard_map/reduce_scatter | solution.py:94
  181.6 1.4 copy-start.19
  186.2 36.7 %copy-start.5 = (bf16[392,768]{1,0:T(8,128)(2,1)S(1)}, bf16[392,768]{1,0:T(8,128)(2,1)}, u32[]{:S(2)}) copy-start(bf16[392,768]{1,0:T(8,128)(2,1)} %reduce-scatter.5.cloned.1.call-done) | copy-start | bytes 1806340
  186.2 36.7 %copy-start.41 = (f32[768]{0:T(1024)S(1)}, f32[768]{0:T(1024)}, u32[]{:S(2)}) copy-start(f32[768]{0:T(1024)} %param.34) | copy-start | bytes 9220
  186.2 64.8 %all-gather.11.cloned.1.call-start = ((), (), s32[]{:S(2)}) async-start(), calls=%async_computation.10 | async-start | bytes 1806336 | tf_op jit(solution)/shard_map/all_gather | solution.py:126
  227.8 151.5 %reduce-scatter.11.cloned.1.call-start = ((), (), s32[]{:S(2)}) async-start(), calls=%async_computation.11 | async-start | bytes 1806336 | tf_op jit(solution)/shard_map/reduce_scatter | solution.py:165
  254.4 6.5 %copy-start.9 = (bf16[784,384]{0,1:T(8,128)(2,1)S(1)}, bf16[784,384]{0,1:T(8,128)(2,1)}, u32[]{:S(2)}) copy-start(bf16[784,384]{0,1:T(8,128)(2,1)} %copy.47) | copy-start | bytes 1806340
  254.4 6.5 %copy-start.10 = (bf16[784,384]{0,1:T(8,128)(2,1)S(1)}, bf16[784,384]{0,1:T(8,128)(2,1)}, u32[]{:S(2)}) copy-start(bf16[784,384]{0,1:T(8,128)(2,1)} %copy.51) | copy-start | bytes 1806340
  260.9 28.9 %copy-start.13 = (bf16[6,64,784]{2,1,0:T(8,128)(2,1)}, bf16[6,64,784]{2,1,0:T(8,128)(2,1)S(1)}, u32[]{:S(2)}) copy-start(bf16[6,64,784]{2,1,0:T(8,128)(2,1)S(1)} %convolution_convert_fusion.4) | copy-start | bytes 1806340
  273.0 12.3 %copy-start.6 = (bf16[784,384]{0,1:T(8,128)(2,1)S(1)}, bf16[784,384]{0,1:T(8,128)(2,1)}, u32[]{:S(2)}) copy-start(bf16[784,384]{0,1:T(8,128)(2,1)} %copy.48) | copy-start | bytes 1806340
  285.3 2.8 copy-start.7
  288.1 1.7 copy-start.15
  289.8 0.9 copy-start.17
  295.1 290.3 %all-reduce.5.cloned.1.call-start = ((), (), s32[]{:S(2)}) async-start(), calls=%async_computation.12 | async-start | bytes 28311552 | tf_op jit(solution)/shard_map/psum | solution.py:253
  295.4 7.0 %copy-start.20 = (bf16[784,1536]{1,0:T(8,128)(2,1)S(1)}, bf16[784,1536]{1,0:T(8,128)(2,1)}, u32[]{:S(2)}) copy-start(bf16[784,1536]{1,0:T(8,128)(2,1)} %copy-done.19) | copy-start | bytes 7225348
  295.4 7.0 %copy-start.45 = (bf16[784,768]{1,0:T(8,128)(2,1)S(1)}, bf16[784,768]{1,0:T(8,128)(2,1)}, u32[]{:S(2)}) copy-start(bf16[784,768]{1,0:T(8,128)(2,1)} %all-gather.9.cloned.1.call-done) | copy-start | bytes 3612676
  302.5 4.4 copy-start.26
  302.5 4.4 copy-start.46
  306.8 1.8 copy-start.14
  306.8 1.8 copy-start.16
  306.9 1.8 copy-start.18
  306.9 2.4 copy-start.44
  313.3 66.1 %copy-start.32 = (f32[392]{0:T(512)S(1)}, f32[392]{0:T(512)}, u32[]{:S(2)}) copy-start(f32[392]{0:T(512)} %copy-done.31) | copy-start | bytes 4708
  313.3 66.1 %copy-start.33 = (f32[768]{0:T(1024)S(1)}, f32[768]{0:T(1024)}, u32[]{:S(2)}) copy-start(f32[768]{0:T(1024)} %param.20) | copy-start | bytes 9220
  313.4 67.7 %copy-start.38 = (f32[392]{0:T(512)S(1)}, f32[392]{0:T(512)}, u32[]{:S(2)}) copy-start(f32[392]{0:T(512)} %copy-done.37) | copy-start | bytes 4708
  313.4 67.7 %copy-start.36 = (f32[392]{0:T(512)S(1)}, f32[392]{0:T(512)}, u32[]{:S(2)}) copy-start(f32[392]{0:T(512)} %copy-done.35) | copy-start | bytes 4708
  379.4 3.5 copy-start.11
  585.4 2.5 copy-start.24
  585.4 3.5 copy-start.23
  585.4 4.5 copy-start.22
  587.9 3.6 copy-start.12
  590.0 3.8 slice-start
  591.5 2.5 slice-start.1
  594.0 3.4 copy-start.1
Sparse Core Ops, SparseCore 0:
  12.4 25.7 all-gather.4
  82.6 22.0 reduce-scatter.4
  108.9 23.0 all-gather.6
  133.4 23.0 all-gather.8
  176.7 22.0 reduce-scatter.8
  200.8 22.0 reduce-scatter.6
  228.0 23.0 all-gather.10
  295.3 22.0 reduce-scatter.10
  323.6 261.7 all-reduce.4
where the time goes:
time: 613 us; the launch traced here: 604 us
  waiting for transfers between devices  303 us (49%)
  blocking collectives  103 us (17%)
  matrix products  90.6 us (15%)
  other arithmetic  60.8 us (10%)
  local copies, waits for them, and re-layouts  31.1 us (5%)
  between operations  14.8 us (2%)
    psum x1, waiting for transfers between devices, local(): lax.psum((grad_wquery, grad_bquery, grad_wkey, grad_wvalue, grad_bvalue,...  161 us
    psum x1, blocking collectives, local(): lax.psum((grad_wquery, grad_bquery, grad_wkey, grad_wvalue, grad_bvalue,...  64 us
    psum x1, blocking collectives, local(): lax.psum((grad_gain1, grad_shift1, grad_boutput, grad_gain2, grad_shift2,...  39.1 us
    all_gather x1, waiting for transfers between devices, head_layer(): grad_columns = lax.all_gather(grad_branch, 'mp', axis=0, tiled=True)  23 us
    all_gather x1, waiting for transfers between devices, head_layer(): gathered2 = lax.all_gather(normed2, 'mp', axis=0, tiled=True)  22.6 us
    reduce_scatter x1, waiting for transfers between devices, head_layer(): lax.psum_scatter(jnp.dot(part_rows, w_down, preferred_element_type=jnp.fl...  22.3 us
    reduce_scatter x1, waiting for transfers between devices, head_layer(): lax.psum_scatter(jnp.dot(part_rows, w_output, preferred_element_type=jnp....  22.1 us
    all_gather x1, waiting for transfers between devices, head_layer(): gathered1 = lax.all_gather(normed1, 'mp', axis=0, tiled=True)  21.1 us
  transfers between devices with their start and end apart: 9, of which 8 were waited for; matrix products, arithmetic and copies ran while one was open for 8% of the time, Pallas kernels for 0%

commit v1 on v0

--- a/solution.py
+++ b/solution.py
@@ -6,6 +6,27 @@
 HEAD = 64
 epsilon = 1e-06
 masked_score = -1e30
+
+
+def laid_out(pieces, dim):
+    pieces = jnp.moveaxis(pieces, 0, dim)
+    shape = pieces.shape
+    return pieces.reshape(*shape[:dim], shape[dim] * shape[dim + 1], *shape[dim + 2 :])
+
+
+def collected_by_bits(x, axis):
+    size, mine = (lax.axis_size(axis), lax.axis_index(axis))
+    parts, distance = (x[None], 1)
+    while distance < size:
+        received = lax.ppermute(parts, axis, [(i, i ^ distance) for i in range(size)])
+        low = mine & distance == 0
+        parts = jnp.concatenate([jnp.where(low, parts, received), jnp.where(low, received, parts)])
+        distance *= 2
+    return parts
+
+
+def collect(shard, axis, dim):
+    return laid_out(collected_by_bits(shard, axis), dim)
 
 
 def normalize(values, gain, shift):
@@ -123,7 +144,7 @@
     grad_bdown = jnp.sum(cotangent_f, axis=0)
     grad_branch = grad_hidden.astype(jnp.bfloat16)
     grad_boutput = jnp.sum(grad_branch.astype(jnp.float32), axis=0)
-    grad_columns = lax.all_gather(grad_branch, "mp", axis=0, tiled=True)
+    grad_columns = collect(grad_branch, "mp", 0)
     grad_woutput = jnp.einsum(
         "gc,gd->cd", context, grad_columns, preferred_element_type=jnp.float32
     )

time: 613 us -> 606 us (0.989)
  waiting for transfers between devices: 303 us -> 296 us
    all_gather x1 -> x0, waiting for transfers between devices: 23 us -> none  [head_layer(): grad_columns = lax.all_gather(grad_branch, 'mp', axis=0, tiled=True)]
    ppermute x0 -> x1, waiting for transfers between devices: none -> 15.1 us  [collected_by_bits(): lax.ppermute(parts, axis, [(i, i ^ distance) for i in range(size)])]
    unnamed x108 -> x112, local copies, waits for them, and re-layouts: 20.5 us -> 21.6 us
where the time goes in v1:
time: 606 us; the launch traced here: 597 us
  waiting for transfers between devices  296 us (49%)
  blocking collectives  102 us (17%)
  matrix products  89.5 us (15%)
  other arithmetic  61.3 us (10%)
  local copies, waits for them, and re-layouts  32.2 us (5%)
  between operations  14.8 us (2%)
    psum x1, waiting for transfers between devices, local(): lax.psum((grad_wquery, grad_bquery, grad_wkey, grad_wvalue, grad_bvalue,...  162 us
    psum x1, blocking collectives, local(): lax.psum((grad_wquery, grad_bquery, grad_wkey, grad_wvalue, grad_bvalue,...  63 us
    psum x1, blocking collectives, local(): lax.psum((grad_gain1, grad_shift1, grad_boutput, grad_gain2, grad_shift2,...  39.1 us
    all_gather x1, waiting for transfers between devices, head_layer(): gathered2 = lax.all_gather(normed2, 'mp', axis=0, tiled=True)  22.6 us
    reduce_scatter x1, waiting for transfers between devices, head_layer(): lax.psum_scatter(jnp.dot(part_rows, w_down, preferred_element_type=jnp.fl...  22.3 us
    reduce_scatter x1, waiting for transfers between devices, head_layer(): lax.psum_scatter(jnp.dot(part_rows, w_output, preferred_element_type=jnp....  22.1 us
    unnamed x112, local copies, waits for them, and re-layouts  21.6 us
    all_gather x1, waiting for transfers between devices, head_layer(): gathered1 = lax.all_gather(normed1, 'mp', axis=0, tiled=True)  21.1 us
  transfers between devices with their start and end apart: 9, of which 8 were waited for; matrix products, arithmetic and copies ran while one was open for 8% of the time, Pallas kernels for 0%

profile of v1, /device:TPU:0, one launch (start us, length us, event | category | flops | bytes accessed | tf_op | source)
XLA Modules:
  0.0 597.0 jit_solution(5678503648696808166)
XLA Ops:
  7.3 1.4 convert_reduce_fusion.4
  8.7 1.4 fusion.22
  10.1 2.2 fusion.20
  12.4 1.3 pad_maximum_fusion.2
  14.5 0.9 constant_dynamic-update-slice_fusion.2
  17.1 21.1 %all-gather.4.cloned.1.call-done = bf16[784,768]{1,0:T(8,128)(2,1)} async-done(((bf16[392,768]{1,0:T(8,128)(2,1)}), bf16[784,768]{1,0:T(8,128)(2,1)}) %all-gather.4.cloned.1.call-update) | async-done | bytes 1204240 | tf_op jit(solution)/shard_map/all_gather | solution.py:72
  38.2 3.5 fusion.8
  41.8 1.2 fusion.37
  43.0 2.2 copy.47
  45.2 2.2 copy.48
  47.4 1.1 copy.49
  48.5 10.4 %fusion = (f32[6,784]{1,0:T(8,128)S(1)}, f32[6,784,784]{1,2,0:T(8,128)}) fusion(pred[784]{0:T(1024)(128)(4,1)S(1)} %compare_reduce_fusion, bf16[784,6,64]{0,2,1:T(8,128)(2,1)} %bitcast.62, bf16[784,6,64]{0,2,1:T(8,128)(2,1)} %bitcast.64), kind=kOutput, calls=%fused_computation.5 | convolution fusion | flops 483114912 | bytes 15975568 | tf_op jit(solution)/shard_map/ipha,iqha->ihpq/dot_general | solution.py:85
  58.9 9.3 %exponential_reduce_fusion = f32[6,784]{1,0:T(8,128)S(1)} fusion(f32[6,784,784]{1,2,0:T(8,128)} %get-tuple-element.60, f32[6,784]{1,0:T(8,128)S(1)} %get-tuple-element.59, pred[784]{0:T(1024)(128)(4,1)S(1)} %compare_reduce_fusion), kind=kLoop, calls=%fused_computation.3 | loop fusion | flops 14747040 | bytes 14790160 | tf_op jit(solution)/shard_map/reduce_sum | solution.py:92
  68.2 8.2 %fusion.1 = bf16[6,784,784]{1,2,0:T(8,128)(2,1)S(1)} fusion(f32[6,784,784]{1,2,0:T(8,128)} %get-tuple-element.60, f32[6,784]{1,0:T(8,128)S(1)} %log_add_fusion, pred[784]{0:T(1024)(128)(4,1)S(1)} %compare_reduce_fusion), kind=kLoop, calls=%fused_computation.6 | loop fusion | flops 14751744 | bytes 22147216 | tf_op jit(solution)/shard_map/convert_element_type | solution.py:93
  76.5 1.7 convolution_convert_fusion.5
  78.2 1.5 copy-done.2
  80.6 1.8 convolution_convert_fusion.1
  82.5 22.1 %reduce-scatter.5.cloned.1.call-done = bf16[392,768]{1,0:T(8,128)(2,1)} async-done(((bf16[784,768]{1,0:T(8,128)(2,1)}), bf16[392,768]{1,0:T(8,128)(2,1)}) %reduce-scatter.5.cloned.1.call-update) | async-done | bytes 602128 | tf_op jit(solution)/shard_map/reduce_scatter | solution.py:100
  104.7 1.4 fusion.27
  106.1 1.4 multiply_reduce_fusion.1
  107.6 1.2 add_convert_fusion.2
  109.4 22.6 %all-gather.6.cloned.1.call-done = bf16[784,768]{1,0:T(8,128)(2,1)} async-done(((bf16[392,768]{1,0:T(8,128)(2,1)}), bf16[784,768]{1,0:T(8,128)(2,1)}) %all-gather.6.cloned.1.call-update) | async-done | bytes 1204240 | tf_op jit(solution)/shard_map/all_gather | solution.py:110
  132.0 6.3 %fusion.39 = f32[784,1536]{1,0:T(8,128)} fusion(bf16[784,768]{1,0:T(8,128)(2,1)} %all-gather.6.cloned.1.call-done, bf16[768,1536]{1,0:T(8,128)(2,1)} %param.31), kind=kOutput, calls=%fused_computation.101 | convolution fusion | flops 1849688064 | bytes 8380416 | tf_op jit(solution)/shard_map/dot_general | solution.py:111
  138.3 18.2 %all-gather.8.cloned.1.call-done = bf16[784,768]{1,0:T(8,128)(2,1)} async-done(((bf16[392,768]{1,0:T(8,128)(2,1)}), bf16[784,768]{1,0:T(8,128)(2,1)}) %all-gather.8.cloned.1.call-update) | async-done | bytes 1204240 | tf_op jit(solution)/shard_map/all_gather | solution.py:124
  156.5 15.6 %convert_reduce_fusion = (f32[1536]{0:T(1024)S(1)}, bf16[784,1536]{1,0:T(8,128)(2,1)S(1)}, f32[784,1536]{1,0:T(8,128)}) fusion(f32[784,1536]{1,0:T(8,128)} %fusion.39, f32[1536]{0:T(1024)S(1)} %copy-done.41, bf16[784,768]{1,0:T(8,128)(2,1)} %all-gather.8.cloned.1.call-done, bf16[1536,768]{1,0:T(8,128)(2,1)S(1)} %copy-done), kind=kOutput, calls=%fused_computation.9 | convolution fusion | flops 1940003328 | bytes 15618048 | tf_op jit(solution)/shard_map/gd,fd->gf/dot_general | solution.py:126
  172.1 1.4 copy-done.21
  173.5 3.1 convolution_convert_fusion.2
  176.8 5.0 multiply_convert_fusion.1
  181.9 1.4 copy-done.19
  183.3 3.1 convolution_convert_fusion.3
  186.5 12.2 %reduce-scatter.9.cloned.1.call-done = bf16[392,768]{1,0:T(8,128)(2,1)} async-done(((bf16[784,768]{1,0:T(8,128)(2,1)}), bf16[392,768]{1,0:T(8,128)(2,1)}) %reduce-scatter.9.cloned.1.call-update) | async-done | bytes 602128 | tf_op jit(solution)/shard_map/reduce_scatter | solution.py:132
  198.8 1.9 fusion.24
  200.7 22.3 %reduce-scatter.7.cloned.1.call-done = bf16[392,768]{1,0:T(8,128)(2,1)} async-done(((bf16[784,768]{1,0:T(8,128)(2,1)}), bf16[392,768]{1,0:T(8,128)(2,1)}) %reduce-scatter.7.cloned.1.call-update) | async-done | bytes 602128 | tf_op jit(solution)/shard_map/reduce_scatter | solution.py:115
  222.9 2.7 fusion.35
  225.7 1.3 convert_reduce_fusion.6
  227.4 15.1 %collective-permute-done = bf16[1,392,768]{2,1,0:T(8,128)(2,1)} collective-permute-done((bf16[1,392,768]{2,1,0:T(8,128)(2,1)S(1)}, bf16[1,392,768]{2,1,0:T(8,128)(2,1)}, u32[]{:S(2)}, u32[]{:S(2)}) %collective-permute-start) | collective-permute-done | bytes 602144 | tf_op jit(solution)/shard_map/ppermute | solution.py:21
  242.5 1.2 broadcast_select_fusion.1
  243.8 1.0 copy-done.22
  245.7 1.1 copy.51
  246.8 6.4 %convolution_convert_fusion.4 = bf16[6,64,784]{2,1,0:T(8,128)(2,1)S(1)} fusion(bf16[784,6,64]{0,2,1:T(8,128)(2,1)} %bitcast.68, bf16[6,784,784]{1,2,0:T(8,128)(2,1)} %copy-done.2), kind=kOutput, calls=%fused_computation.57 | convolution fusion | flops 472356864 | bytes 8580096 | tf_op jit(solution)/shard_map/ihpq,ipha->iqha/dot_general | solution.py:159
  253.3 12.2 %multiply_reduce_fusion = (f32[6,784]{1,0:T(8,128)S(1)}, f32[6,784,784]{1,2,0:T(8,128)}) fusion(f32[6,784,784]{1,2,0:T(8,128)} %get-tuple-element.60, f32[6,784]{1,0:T(8,128)S(1)} %log_add_fusion, pred[784]{0:T(1024)(128)(4,1)S(1)} %compare_reduce_fusion, bf16[784,6,64]{0,2,1:T(8,128)(2,1)S(1)} %bitcast.69, bf16[784,6,64]{0,2,1:T(8,128)(2,1)S(1)} %bitcast.67), kind=kOutput, calls=%fused_computation.1 | convolution fusion | flops 490490784 | bytes 30746128 | tf_op jit(solution)/shard_map/ipha,iqha->ihpq/dot_general | solution.py:156
  265.5 12.3 %multiply_convert_fusion = bf16[6,784,784]{1,2,0:T(8,128)(2,1)S(1)} fusion(f32[6,784,784]{1,2,0:T(8,128)} %get-tuple-element.62, f32[6,784,784]{1,2,0:T(8,128)} %get-tuple-element.60, f32[6,784]{1,0:T(8,128)S(1)} %get-tuple-element.61, f32[6,784]{1,0:T(8,128)S(1)} %log_add_fusion, pred[784]{0:T(1024)(128)(4,1)S(1)} %compare_reduce_fusion), kind=kLoop, calls=%fused_computation | loop fusion | flops 22127616 | bytes 36917776 | tf_op jit(solution)/shard_map/convert_element_type | solution.py:166
  277.8 2.8 fusion.17
  280.6 1.7 fusion.16
  283.2 4.5 convolution_convert_fusion
  287.7 7.0 %fusion.41 = f32[768,1536]{1,0:T(8,128)} fusion(bf16[784,768]{1,0:T(8,128)(2,1)} %all-gather.6.cloned.1.call-done, bf16[784,1536]{1,0:T(8,128)(2,1)} %copy-done.21), kind=kOutput, calls=%fused_computation.103 | convolution fusion | flops 1849688064 | bytes 8331264 | tf_op jit(solution)/shard_map/gd,gf->df/dot_general | solution.py:129
  294.8 4.5 fusion.42
  299.3 1.8 fusion.40
  301.7 2.2 fusion.32
  303.9 1.9 fusion.36
  305.8 1.9 convert_reduce_fusion.1
  307.7 63.0 %all-reduce.1 = (f32[384]{0:T(512)}, f32[384]{0:T(512)}, f32[1536]{0:T(1024)}) all-reduce(f32[384]{0:T(512)S(1)} %get-tuple-element.58, f32[384]{0:T(512)S(1)} %get-tuple-element.57, f32[1536]{0:T(1024)S(1)} %get-tuple-element.39), channel_id=1, replica_groups=mesh['dp'=16,'mp'=2] {'dp'}, use_global_device_ids=true, to_apply=%region_21.22 | all-reduce | flops 2304 | bytes 18432 | tf_op jit(solution)/shard_map/psum | solution.py:274
  370.7 1.6 convert_reduce_fusion.2
  372.4 1.8 fusion.25
  374.2 2.7 convert_reduce_fusion.5
  376.9 39.1 %all-reduce = (f32[768]{0:T(1024)}, f32[768]{0:T(1024)}, f32[768]{0:T(1024)}, f32[768]{0:T(1024)}, f32[768]{0:T(1024)}, /*index=5*/f32[768]{0:T(1024)}) all-reduce(f32[768]{0:T(1024)S(1)} %get-tuple-element.19, f32[768]{0:T(1024)S(1)} %get-tuple-element.22, ...), channel_id=1, replica_groups=mesh['dp'=16,'mp'=2] {'dp','mp'}, use_global_device_ids=true, to_apply=%region_16.17 | all-reduce | flops 4608 | bytes 36864 | tf_op jit(solution)/shard_map/psum | solution.py:289
  416.1 161.8 %all-reduce.5.cloned.1.call-done = (f32[768,384]{1,0:T(8,128)}, f32[768,384]{1,0:T(8,128)}, f32[768,384]{1,0:T(8,128)}, f32[384,768]{1,0:T(8,128)}, f32[768,1536]{1,0:T(8,128)}, /*index=5*/f32[1536,768]{1,0:T(8,128)}) async-done(((f32[768,384]{1,0:T(8,128)}, f32[768,384]{1,0:T(8,128)}, f32[768,384]{1,0:T(8,128)}, f32[384,768]{1,0:T(8,128)}, f32[768,1536]{1,0:T(8,128)}, /*index=5*/f32[1536,768]{1,0:T(8,128)}), ...) | async-done | bytes 14155792 | tf_op jit(solution)/shard_map/psum | solution.py:274
  577.9 2.5 copy.67
  580.5 1.0 copy.68
  581.5 1.0 copy.69
  582.5 1.0 copy.70
  584.1 2.2 copy.71
  586.6 2.4 copy.72
  589.0 1.0 copy-done.1
  (134 shorter events, 8.4 us)
Async XLA Ops:
  7.2 149.3 %copy-start = (bf16[1536,768]{1,0:T(8,128)(2,1)S(1)}, bf16[1536,768]{1,0:T(8,128)(2,1)}, u32[]{:S(2)}) copy-start(bf16[1536,768]{1,0:T(8,128)(2,1)} %param.33) | copy-start | bytes 7077892
  7.2 5.2 copy-start.44
  7.2 7.2 %copy-start.29 = (bf16[768,384]{1,0:T(8,128)(2,1)S(1)}, bf16[768,384]{1,0:T(8,128)(2,1)}, u32[]{:S(2)}) copy-start(bf16[768,384]{1,0:T(8,128)(2,1)} %param.22) | copy-start | bytes 1769476
  7.2 8.1 %copy-start.30 = (bf16[768,384]{1,0:T(8,128)(2,1)S(1)}, bf16[768,384]{1,0:T(8,128)(2,1)}, u32[]{:S(2)}) copy-start(bf16[768,384]{1,0:T(8,128)(2,1)} %param.24) | copy-start | bytes 1769476
  7.2 31.0 %all-gather.4.cloned.1.call-start = ((), (), s32[]{:S(2)}) async-start(), calls=%async_computation.4 | async-start | bytes 1806336 | tf_op jit(solution)/shard_map/all_gather | solution.py:72
  8.7 7.5 %copy-start.33 = (f32[392]{0:T(512)}, f32[392]{0:T(512)S(1)}, u32[]{:S(2)}) copy-start(f32[392]{0:T(512)S(1)} %broadcast_multiply_fusion.1) | copy-start | bytes 4708
  10.1 7.0 %copy-start.39 = (f32[392]{0:T(512)}, f32[392]{0:T(512)S(1)}, u32[]{:S(2)}) copy-start(f32[392]{0:T(512)S(1)} %fusion.22) | copy-start | bytes 4708
  10.1 7.0 %copy-start.37 = (f32[392]{0:T(512)}, f32[392]{0:T(512)S(1)}, u32[]{:S(2)}) copy-start(f32[392]{0:T(512)S(1)} %fusion.30) | copy-start | bytes 4708
  12.3 92.3 %reduce-scatter.5.cloned.1.call-start = ((), (), s32[]{:S(2)}) async-start(), calls=%async_computation.5 | async-start | bytes 1806336 | tf_op jit(solution)/shard_map/reduce_scatter | solution.py:100
  12.4 3.9 copy-start.31
  68.2 8.3 %copy-start.8 = (bf16[784,384]{0,1:T(8,128)(2,1)S(1)}, bf16[784,384]{0,1:T(8,128)(2,1)}, u32[]{:S(2)}) copy-start(bf16[784,384]{0,1:T(8,128)(2,1)} %copy.47) | copy-start | bytes 1806340
  76.5 3.3 copy-start.2
  76.5 4.1 copy-start.48
  79.7 0.9 copy-start.27
  79.7 24.9 %copy-start.3 = (bf16[392,768]{1,0:T(8,128)(2,1)S(1)}, bf16[392,768]{1,0:T(8,128)(2,1)}, u32[]{:S(2)}) copy-start(bf16[392,768]{1,0:T(8,128)(2,1)} %param.18) | copy-start | bytes 1806340
  79.8 24.9 %copy-start.32 = (f32[768]{0:T(1024)S(1)}, f32[768]{0:T(1024)}, u32[]{:S(2)}) copy-start(f32[768]{0:T(1024)} %param.28) | copy-start | bytes 9220
  82.5 25.1 %copy-start.36 = (f32[768]{0:T(1024)S(1)}, f32[768]{0:T(1024)}, u32[]{:S(2)}) copy-start(f32[768]{0:T(1024)} %param.29) | copy-start | bytes 9220
  82.5 25.1 %copy-start.42 = (f32[768]{0:T(1024)S(1)}, f32[768]{0:T(1024)}, u32[]{:S(2)}) copy-start(f32[768]{0:T(1024)} %param.30) | copy-start | bytes 9220
  82.5 49.5 %all-gather.6.cloned.1.call-start = ((), (), s32[]{:S(2)}) async-start(), calls=%async_computation.6 | async-start | bytes 1806336 | tf_op jit(solution)/shard_map/all_gather | solution.py:110
  104.7 2.9 copy-start.4
  108.8 47.7 %all-gather.8.cloned.1.call-start = ((), (), s32[]{:S(2)}) async-start(), calls=%async_computation.8 | async-start | bytes 1806336 | tf_op jit(solution)/shard_map/all_gather | solution.py:124
  109.3 47.1 %copy-start.41 = (f32[1536]{0:T(1024)S(1)}, f32[1536]{0:T(1024)}, u32[]{:S(2)}) copy-start(f32[1536]{0:T(1024)} %param.32) | copy-start | bytes 18436
  109.3 89.4 %reduce-scatter.9.cloned.1.call-start = ((), (), s32[]{:S(2)}) async-start(), calls=%async_computation.9 | async-start | bytes 1806336 | tf_op jit(solution)/shard_map/reduce_scatter | solution.py:132
  156.5 17.0 %copy-start.45 = (bf16[768,1536]{1,0:T(8,128)(2,1)S(1)}, bf16[768,1536]{1,0:T(8,128)(2,1)}, u32[]{:S(2)}) copy-start(bf16[768,1536]{1,0:T(8,128)(2,1)} %param.31) | copy-start | bytes 7077892
  172.1 1.4 copy-start.21
  176.6 46.3 %reduce-scatter.7.cloned.1.call-start = ((), (), s32[]{:S(2)}) async-start(), calls=%async_computation.7 | async-start | bytes 1806336 | tf_op jit(solution)/shard_map/reduce_scatter | solution.py:115
  181.9 1.4 copy-start.19
  186.4 36.5 %copy-start.5 = (bf16[392,768]{1,0:T(8,128)(2,1)S(1)}, bf16[392,768]{1,0:T(8,128)(2,1)}, u32[]{:S(2)}) copy-start(bf16[392,768]{1,0:T(8,128)(2,1)} %reduce-scatter.5.cloned.1.call-done) | copy-start | bytes 1806340
  186.4 36.5 %copy-start.43 = (f32[768]{0:T(1024)S(1)}, f32[768]{0:T(1024)}, u32[]{:S(2)}) copy-start(f32[768]{0:T(1024)} %param.34) | copy-start | bytes 9220
  186.5 184.3 %reduce-scatter.11.cloned.1.call-start = ((), (), s32[]{:S(2)}) async-start(), calls=%async_computation.10 | async-start | bytes 1806336 | tf_op jit(solution)/shard_map/reduce_scatter | solution.py:186
  227.0 15.5 %collective-permute-start = (bf16[1,392,768]{2,1,0:T(8,128)(2,1)S(1)}, bf16[1,392,768]{2,1,0:T(8,128)(2,1)}, u32[]{:S(2)}, u32[]{:S(2)}) collective-permute-start(bf16[1,392,768]{2,1,0:T(8,128)(2,1)S(1)} %bitcast.81), channel_id=1, source_target_pairs={{0,1},{1,0},{2,3},{3,2},{4,5},{5,4},{6,7},{7,6},{8,9},{9,8},{10,11... | collective-permute-start | bytes 1806344 | tf_op jit(solution)/shard_map/ppermute | solution.py:21
  227.4 17.4 %copy-start.49 = (bf16[384,768]{1,0:T(8,128)(2,1)S(1)}, bf16[384,768]{1,0:T(8,128)(2,1)}, u32[]{:S(2)}) copy-start(bf16[384,768]{1,0:T(8,128)(2,1)} %param.27) | copy-start | bytes 1769476
  243.8 1.0 copy-start.22
  246.8 6.5 %copy-start.9 = (bf16[784,384]{0,1:T(8,128)(2,1)S(1)}, bf16[784,384]{0,1:T(8,128)(2,1)}, u32[]{:S(2)}) copy-start(bf16[784,384]{0,1:T(8,128)(2,1)} %copy.47) | copy-start | bytes 1806340
  246.8 6.5 %copy-start.10 = (bf16[784,384]{0,1:T(8,128)(2,1)S(1)}, bf16[784,384]{0,1:T(8,128)(2,1)}, u32[]{:S(2)}) copy-start(bf16[784,384]{0,1:T(8,128)(2,1)} %copy.51) | copy-start | bytes 1806340
  253.3 29.0 %copy-start.13 = (bf16[6,64,784]{2,1,0:T(8,128)(2,1)}, bf16[6,64,784]{2,1,0:T(8,128)(2,1)S(1)}, u32[]{:S(2)}) copy-start(bf16[6,64,784]{2,1,0:T(8,128)(2,1)S(1)} %convolution_convert_fusion.4) | copy-start | bytes 1806340
  265.5 12.3 %copy-start.6 = (bf16[784,384]{0,1:T(8,128)(2,1)S(1)}, bf16[784,384]{0,1:T(8,128)(2,1)}, u32[]{:S(2)}) copy-start(bf16[784,384]{0,1:T(8,128)(2,1)} %copy.48) | copy-start | bytes 1806340
  277.8 2.8 copy-start.7
  280.6 1.7 copy-start.15
  282.3 0.9 copy-start.17
  287.6 290.3 %all-reduce.5.cloned.1.call-start = ((), (), s32[]{:S(2)}) async-start(), calls=%async_computation.11 | async-start | bytes 28311552 | tf_op jit(solution)/shard_map/psum | solution.py:274
  287.7 7.0 %copy-start.20 = (bf16[784,1536]{1,0:T(8,128)(2,1)S(1)}, bf16[784,1536]{1,0:T(8,128)(2,1)}, u32[]{:S(2)}) copy-start(bf16[784,1536]{1,0:T(8,128)(2,1)} %copy-done.19) | copy-start | bytes 7225348
  287.7 7.0 %copy-start.47 = (bf16[784,768]{1,0:T(8,128)(2,1)S(1)}, bf16[784,768]{1,0:T(8,128)(2,1)}, u32[]{:S(2)}) copy-start(bf16[784,768]{1,0:T(8,128)(2,1)} %all-gather.8.cloned.1.call-done) | copy-start | bytes 3612676
  294.7 4.5 copy-start.23
  294.7 4.5 copy-start.28
  299.3 1.8 copy-start.14
  299.3 1.8 copy-start.16
  299.3 1.8 copy-start.18
  299.3 2.4 copy-start.46
  305.7 65.0 %copy-start.34 = (f32[392]{0:T(512)S(1)}, f32[392]{0:T(512)}, u32[]{:S(2)}) copy-start(f32[392]{0:T(512)} %copy-done.33) | copy-start | bytes 4708
  305.7 65.0 %copy-start.35 = (f32[768]{0:T(1024)S(1)}, f32[768]{0:T(1024)}, u32[]{:S(2)}) copy-start(f32[768]{0:T(1024)} %param.20) | copy-start | bytes 9220
  305.8 66.6 %copy-start.40 = (f32[392]{0:T(512)S(1)}, f32[392]{0:T(512)}, u32[]{:S(2)}) copy-start(f32[392]{0:T(512)} %copy-done.39) | copy-start | bytes 4708
  305.8 66.6 %copy-start.38 = (f32[392]{0:T(512)S(1)}, f32[392]{0:T(512)}, u32[]{:S(2)}) copy-start(f32[392]{0:T(512)} %copy-done.37) | copy-start | bytes 4708
  370.7 3.5 copy-start.11
  577.9 2.5 copy-start.26
  577.9 3.5 copy-start.25
  577.9 4.5 copy-start.24
  580.4 3.6 copy-start.12
  582.5 3.8 slice-start
  584.1 2.5 slice-start.1
  586.6 3.4 copy-start.1
Sparse Core Ops, SparseCore 0:
  12.4 25.7 all-gather.3
  82.6 22.0 reduce-scatter.4
  108.9 23.0 all-gather.5
  133.4 23.0 all-gather.7
  176.7 22.0 reduce-scatter.8
  200.9 22.0 reduce-scatter.6
  287.8 22.0 reduce-scatter.10
  316.1 261.7 all-reduce.4
